TPU v7x, 128 devices: a whole 4x4x4 slice. The times are simulated.
128 devices in a mesh: seq: 16 (over y, x_hi, core), head: 8 (over z, x_lo).
Axes of the slice: x: 4 (x_hi: 2, x_lo: 2; x = x_hi * 2 + x_lo), y: 4, z: 4, core: 2. Of those that a mesh axis runs over, the one named last changes fastest.
Arguments:
- queries: bfloat16 [2048, 8192], P('seq', 'head'), may hold values from -24 to 24
- key_rows: bfloat16 [2048, 1024], P('seq', 'head'), may hold values from -6 to 6
- value_rows: bfloat16 [2048, 1024], P('seq', 'head'), may hold values from -6 to 6
- out_weight: bfloat16 [8192, 8192], P('head'), may hold values from -0.5 to 0.5
- residual: bfloat16 [2048, 8192], P('seq', 'head'), may hold values from -54 to 54
- norm_gain: float32 [8192], replicated, may hold values from 0.1 to 1.9
- gate_weight: bfloat16 [8192, 28672], P(None, ('seq', 'head')), may hold values from -0.0625 to 0.0625
- up_weight: bfloat16 [8192, 28672], P(None, ('seq', 'head')), may hold values from -0.0625 to 0.0625
Outputs:
- edit_keys: bfloat16 [2048, 28672], P(None, ('seq', 'head'))
- hidden_state: bfloat16 [2048, 8192], P('seq', 'head')
All inputs are finite; a program needn't handle non-finite values.
Results may differ from a plain program's by a relative error of at most 0.019.
Values may be sent and summed in bfloat16 or wider, within the bound.
No kernel may reach another device: no remote copies, remote signals or barrier semaphores. Data moves between devices by JAX's collectives and lax.ppermute only.
A program may use at most 128 MiB of HBM per device.

v0:
```python
import jax
import jax.numpy as jnp
from jax import lax
from jax.sharding import PartitionSpec as P

HD = 128
very_low = -1e30


def attend_block(carry_state, rows, places, key_piece, value_piece, key_places):
    maxima, totals, accumulated = carry_state
    scores = jnp.einsum(
        "rkgd,nkd->kgrn", rows, key_piece, preferred_element_type=jnp.float32
    ) / jnp.sqrt(jnp.float32(HD))
    visible = places[:, None] >= key_places[None, :]
    scores = jnp.where(visible, scores, jnp.float32(very_low))
    new_maxima = jnp.maximum(maxima, jnp.max(scores, axis=-1))
    weights = jnp.exp(scores - new_maxima[..., None])
    totals = jnp.sum(weights, axis=-1)
    products = jnp.einsum(
        "kgrn,nkd->kgrd", weights, value_piece.astype(jnp.float32), precision=lax.Precision.HIGHEST
    )
    accumulated = products
    return (new_maxima, totals, accumulated)


def maybe_attend(current, rows, places, key_piece, value_piece, key_places, first_row):

    def compute(carry_state):
        return attend_block(carry_state, rows, places, key_piece, value_piece, key_places)

    def unchanged(carry_state):
        return carry_state

    return lax.cond(first_row <= places[-1], compute, unchanged, current)


def finish_rows(carry_state, row_count, width):
    maxima, totals, accumulated = carry_state
    result = accumulated / totals[..., None]
    return result.transpose(2, 0, 1, 3).reshape(row_count, width).astype(jnp.bfloat16)


def per_device(
    queries, key_rows, value_rows, out_weight, residual, norm_gain, gate_weight, up_weight
):
    tok_count = queries.shape[0]
    seq_index = lax.axis_index("seq")
    head_index = lax.axis_index("head")
    kv_local = key_rows.shape[1] // HD
    q_local = queries.shape[1] // HD
    group_size = q_local // kv_local
    own_first = seq_index * tok_count
    query_sets = ((queries, own_first + jnp.arange(tok_count, dtype=jnp.int32)),)
    shaped = tuple(
        (
            (rows.reshape(rows.shape[0], kv_local, group_size, HD), places)
            for rows, places in query_sets
        )
    )
    initial = tuple(
        (
            (
                jnp.full((kv_local, group_size, rows.shape[0]), very_low, jnp.float32),
                jnp.zeros((kv_local, group_size, rows.shape[0]), jnp.float32),
                jnp.zeros((kv_local, group_size, rows.shape[0], HD), jnp.float32),
            )
            for rows, places in shaped
        )
    )
    first_row = jnp.int32(0)
    key_piece = lax.all_gather(key_rows, "seq", axis=0, tiled=True).reshape(-1, kv_local, HD)
    value_piece = lax.all_gather(value_rows, "seq", axis=0, tiled=True).reshape(-1, kv_local, HD)
    key_places = jnp.arange(key_piece.shape[0], dtype=jnp.int32)
    updated = []
    for (fold_rows, fold_places), current in zip(shaped, initial):
        updated.append(
            maybe_attend(
                current, fold_rows, fold_places, key_piece, value_piece, key_places, first_row
            )
        )
    final_states = tuple(updated)
    finished = [
        finish_rows(state, rows.shape[0], q_local * HD)
        for state, (rows, places) in zip(final_states, shaped)
    ]
    attended = finished[0]
    projected = jnp.dot(attended, out_weight, preferred_element_type=jnp.float32)
    width_total = out_weight.shape[1]
    width_local = residual.shape[1]
    column_first = head_index * width_local
    shared_sum = lax.psum_scatter(
        projected.astype(jnp.bfloat16), "head", scatter_dimension=1, tiled=True
    ).astype(jnp.float32)
    hidden_state = (residual.astype(jnp.float32) + shared_sum).astype(jnp.bfloat16)
    widened = hidden_state.astype(jnp.float32)
    square_sum = lax.psum(jnp.sum(widened * widened, axis=-1, keepdims=True), "head")
    gain_local = lax.dynamic_slice_in_dim(norm_gain, column_first, width_local, 0)
    normed_local = (
        widened * lax.rsqrt(square_sum / width_total + 1e-05) * gain_local[None, :]
    ).astype(jnp.bfloat16)
    normed_full = lax.all_gather(normed_local, "head", axis=1, tiled=True)
    shard_rows = lax.all_gather(normed_full, "seq", axis=0, tiled=True)
    gate_sums = jnp.dot(shard_rows, gate_weight, preferred_element_type=jnp.float32)
    up_sums = jnp.dot(shard_rows, up_weight, preferred_element_type=jnp.float32)
    edit_keys = (jax.nn.silu(gate_sums) * up_sums).astype(jnp.bfloat16)
    return (edit_keys, hidden_state)


def solution(mesh):
    return jax.shard_map(
        per_device,
        mesh=mesh,
        in_specs=(
            P("seq", "head"),
            P("seq", "head"),
            P("seq", "head"),
            P("head", None),
            P("seq", "head"),
            P(),
            P(None, ("seq", "head")),
            P(None, ("seq", "head")),
        ),
        out_specs=(P(None, ("seq", "head")), P("seq", "head")),
        check_vma=False,
    )
```

profile of v0, /device:TPU:1, one launch (start us, length us, event | category | flops | bytes accessed | tf_op | source)
XLA Modules:
  0.0 428.1 jit_solution(579743415194872696)
XLA Ops:
  7.2 0.0 reduce-scatter.2.cloned.1.call-start
  7.2 0.6 slice.3
  8.5 28.2 %all_gather.12 = bf16[2048,128]{1,0:T(8,128)(2,1)S(1)} all-gather(bf16[128,128]{1,0:T(8,128)(2,1)} %param.11), channel_id=1, replica_groups=mesh['seq'=16,'head'=8] {'seq'}, dimensions={0}, use_global_device_ids=true | all-gather | bytes 557056 | tf_op jit(solution)/shard_map/all_gather | solution.py:72
  36.7 21.8 %all_gather.13 = bf16[2048,128]{1,0:T(8,128)(2,1)S(1)} all-gather(bf16[128,128]{1,0:T(8,128)(2,1)} %param.12), channel_id=1, replica_groups=mesh['seq'=16,'head'=8] {'seq'}, dimensions={0}, use_global_device_ids=true | all-gather | bytes 557056 | tf_op jit(solution)/shard_map/all_gather | solution.py:73
  58.5 8.9 %conditional.1 = (f32[1,8,128]{2,1,0:T(8,128)S(1)}, f32[1,8,128,128]{2,3,1,0:T(8,128)S(1)}) conditional(s32[]{:T(128)} %bitcast.7, () %tuple.16, (s32[128]{0:T(128)S(1)}, s32[2048]{0:T(1024)S(1)}, bf16[128,1024]{1,0:T(8,128)(2,1)}, bf16[2048,128]{1,0:T(8,128)(2,1)S(1)}, bf16[2048,128]{1,0:T(8,128)(2,1)S(1)}) %tuple.17), branch_computations={%region_0.0_spmd, %region_1.4_spmd} | conditional | flops 3779329024 | bytes 28082704 | solution.py:35
  58.5 0.3 broadcast_compare_fusion
  58.8 2.3 fusion.3
  61.1 4.6 %fusion.8 = f32[1,8,128,128]{2,3,1,0:T(8,128)S(1)} fusion(f32[2048,128,8]{1,0,2:T(8,128)S(1)} %get-tuple-element.30, f32[8,128]{1,0:T(8,128)S(1)} %broadcast_maximum_fusion, pred[128,2048]{0,1:T(8,128)(4,1)S(1)} %broadcast_compare_fusion, bf16[2048,128]{1,0:T(8,128)(2,1)S(1)} %get-tuple-element.17), kind=kOutput, calls=%fused_computation.10 | convolution fusion | flops 3227516928 | bytes 9703424 | tf_op jit(solution)/shard_map/cond/branch_1_fun/kgrn,nkd->kgrd/dot_general | solution.py:20
  65.7 1.7 fusion.2
  67.4 0.1 divide_convert_fusion
  67.5 9.6 %convolution_convert_fusion = bf16[128,8192]{1,0:T(8,128)(2,1)} fusion(bf16[128,1024]{0,1:T(8,128)(2,1)S(1)} %bitcast.53, bf16[1024,8192]{1,0:T(8,128)(2,1)} %param.13), kind=kOutput, calls=%fused_computation.20 | convolution fusion | flops 2148532224 | bytes 19136512 | tf_op jit(solution)/shard_map/dot_general | solution.py:88
  77.1 0.0 all-gather.3.cloned.1.call-start
  77.2 0.7 dynamic_slice.3
  77.9 51.4 %reduce-scatter.2.cloned.1.call-done = bf16[128,1024]{1,0:T(8,128)(2,1)} async-done(((bf16[128,8192]{1,0:T(8,128)(2,1)}), bf16[128,1024]{1,0:T(8,128)(2,1)}) %reduce-scatter.2.cloned.1.call-update) | async-done | bytes 262160 | tf_op jit(solution)/shard_map/reduce_scatter | solution.py:92
  129.3 1.1 fusion.19
  130.4 13.3 %psum.7 = f32[128,1]{0,1:T(1,128)S(1)} all-reduce(f32[128,1]{0,1:T(1,128)S(1)} %bitcast.56), channel_id=1, replica_groups=mesh['seq'=16,'head'=8] {'head'}, use_global_device_ids=true, to_apply=%region_6.7 | all-reduce | flops 128 | bytes 1024 | tf_op jit(solution)/shard_map/psum | solution.py:97
  143.7 0.8 fusion.21
  144.6 0.0 all-gather.3.cloned.1.call-update
  144.6 0.2 all-gather.5.cloned.1.call-start
  144.8 54.0 %all-gather.3.cloned.1.call-done = bf16[128,8192]{1,0:T(8,128)(2,1)} async-done(((bf16[128,1024]{1,0:T(8,128)(2,1)}), bf16[128,8192]{1,0:T(8,128)(2,1)}) %all-gather.3.cloned.1.call-update) | async-done | bytes 2097168 | tf_op jit(solution)/shard_map/all_gather | solution.py:102
  198.9 0.0 all-gather.5.cloned.1.call-update
  198.9 188.1 %all-gather.5.cloned.1.call-done = bf16[2048,8192]{1,0:T(8,128)(2,1)} async-done(((bf16[128,8192]{1,0:T(8,128)(2,1)}), bf16[2048,8192]{1,0:T(8,128)(2,1)}) %all-gather.5.cloned.1.call-update) | async-done | bytes 33554448 | tf_op jit(solution)/shard_map/all_gather | solution.py:103
  387.0 17.3 %fusion.22 = f32[2048,224]{0,1:T(8,128)S(1)} fusion(bf16[2048,8192]{1,0:T(8,128)(2,1)} %all-gather.5.cloned.1.call-done, bf16[8192,224]{0,1:T(8,128)(2,1)} %param.16), kind=kOutput, calls=%fused_computation.32 | convolution fusion | flops 7516192768 | bytes 39059456 | tf_op jit(solution)/shard_map/dot_general | solution.py:104
  404.2 17.3 %fusion.18 = bf16[2048,224]{0,1:T(8,128)(2,1)} fusion(bf16[2048,8192]{1,0:T(8,128)(2,1)} %all-gather.5.cloned.1.call-done, bf16[8192,224]{0,1:T(8,128)(2,1)S(1)} %copy-done.2, f32[2048,224]{0,1:T(8,128)S(1)} %fusion.22), kind=kOutput, calls=%fused_computation.22 | convolution fusion | flops 7518945280 | bytes 39976960 | tf_op jit(solution)/shard_map/dot_general | solution.py:105
  (11 shorter events, 0.0 us)
Async XLA Ops:
  7.2 122.1 %reduce-scatter.2.cloned.1.call-start = ((), (), s32[]{:S(2)}) async-start(), calls=%async_computation.1 | async-start | bytes 2359296 | tf_op jit(solution)/shard_map/reduce_scatter | solution.py:92
  67.5 61.8 %copy-start.1 = (bf16[128,1024]{1,0:T(8,128)(2,1)S(1)}, bf16[128,1024]{1,0:T(8,128)(2,1)}, u32[]{:S(2)}) copy-start(bf16[128,1024]{1,0:T(8,128)(2,1)} %param.14) | copy-start | bytes 786436
  77.1 121.7 %all-gather.3.cloned.1.call-start = ((), (), s32[]{:S(2)}) async-start(), calls=%async_computation.2 | async-start | bytes 2359296 | tf_op jit(solution)/shard_map/all_gather | solution.py:102
  130.4 273.8 %copy-start = (bf16[128,1024]{1,0:T(8,128)(2,1)}, bf16[128,1024]{1,0:T(8,128)(2,1)S(1)}, u32[]{:S(2)}) copy-start(bf16[128,1024]{1,0:T(8,128)(2,1)S(1)} %get-tuple-element.28) | copy-start | bytes 786436
  144.6 242.4 %all-gather.5.cloned.1.call-start = ((), (), s32[]{:S(2)}) async-start(), calls=%async_computation.3 | async-start | bytes 35651584 | tf_op jit(solution)/shard_map/all_gather | solution.py:103
  386.9 17.3 %copy-start.2 = (bf16[8192,224]{0,1:T(8,128)(2,1)S(1)}, bf16[8192,224]{0,1:T(8,128)(2,1)}, u32[]{:S(2)}) copy-start(bf16[8192,224]{0,1:T(8,128)(2,1)} %param.17) | copy-start | bytes 11010052
Sparse Core Ops, SparseCore 0:
  77.3 51.9 reduce-scatter.1
  144.7 54.1 all-gather.2
  201.3 185.5 all-gather.4
where the time goes:
time: 428 us
  waiting for transfers between devices  294 us (69%)
  blocking collectives  63.3 us (15%)
  matrix products  51.1 us (12%)
  between operations  14.5 us (3%)
    all_gather x1, waiting for transfers between devices, per_device(): shard_rows = lax.all_gather(normed_full, 'seq', axis=0, tiled=True)  188 us
    all_gather x1, waiting for transfers between devices, per_device(): normed_full = lax.all_gather(normed_local, 'head', axis=1, tiled=True)  54 us
    reduce_scatter x1, waiting for transfers between devices, per_device(): lax.psum_scatter(projected.astype(jnp.bfloat16), 'head', scatter_dimensio...  51.4 us
    all_gather x1, blocking collectives, per_device(): lax.all_gather(key_rows, 'seq', axis=0, tiled=True)  28.2 us
    all_gather x1, blocking collectives, per_device(): lax.all_gather(value_rows, 'seq', axis=0, tiled=True)  21.8 us
    dot_general x1, matrix products, per_device(): up_sums = jnp.dot(shard_rows, up_weight, preferred_element_type=jnp.float32)  17.3 us
    dot_general x1, matrix products, per_device(): jnp.dot(shard_rows, gate_weight, preferred_element_type=jnp.float32)  17.3 us
    psum x1, blocking collectives, per_device(): lax.psum(jnp.sum(widened * widened, axis=-1, keepdims=True), 'head')  13.3 us
  transfers between devices with their start and end apart: 3, of which 3 were waited for; matrix products, arithmetic and copies ran while one was open for 0% of the time, Pallas kernels for 0%

commit v1 on v0

--- a/solution.py
+++ b/solution.py
@@ -70,7 +70,9 @@
     )
     first_row = jnp.int32(0)
     key_piece = lax.all_gather(key_rows, "seq", axis=0, tiled=True).reshape(-1, kv_local, HD)
-    value_piece = lax.all_gather(value_rows, "seq", axis=0, tiled=True).reshape(-1, kv_local, HD)
+    value_piece = jnp.concatenate(
+        lax.all_to_all(jnp.stack([value_rows] * lax.axis_size("seq")), "seq", 0, 0), axis=0
+    ).reshape(-1, kv_local, HD)
     key_places = jnp.arange(key_piece.shape[0], dtype=jnp.int32)
     updated = []
     for (fold_rows, fold_places), current in zip(shaped, initial):

time: 428 us -> 414 us (0.967)
  blocking collectives: 63.3 us -> 40.3 us
  starting transfers between devices: 0.3 us -> 8.56 us
    all_gather x1 -> x0, blocking collectives: 21.8 us -> none  [per_device(): lax.all_gather(value_rows, 'seq', axis=0, tiled=True)]
    all_to_all x0 -> x1, starting transfers between devices: none -> 8.44 us  [per_device(): lax.all_to_all(jnp.stack([value_rows] * lax.axis_size('seq')), 'seq', 0, 0)]
  transfers between devices with their start and end apart: 3 -> 4, of which waited for: 3 -> 3; matrix products, arithmetic and copies ran while one was open for 0% -> 0% of each run, Pallas kernels for 0% -> 0%
where the time goes in v1:
time: 414 us
  waiting for transfers between devices  292 us (71%)
  matrix products  51.1 us (12%)
  blocking collectives  40.3 us (10%)
  between operations  14.5 us (4%)
  starting transfers between devices  8.56 us (2%)
    all_gather x1, waiting for transfers between devices, per_device(): shard_rows = lax.all_gather(normed_full, 'seq', axis=0, tiled=True)  188 us
    all_gather x1, waiting for transfers between devices, per_device(): normed_full = lax.all_gather(normed_local, 'head', axis=1, tiled=True)  54.2 us
    reduce_scatter x1, waiting for transfers between devices, per_device(): lax.psum_scatter(projected.astype(jnp.bfloat16), 'head', scatter_dimensio...  49.8 us
    all_gather x1, blocking collectives, per_device(): lax.all_gather(key_rows, 'seq', axis=0, tiled=True)  26.8 us
    dot_general x1, matrix products, per_device(): up_sums = jnp.dot(shard_rows, up_weight, preferred_element_type=jnp.float32)  17.3 us
    dot_general x1, matrix products, per_device(): jnp.dot(shard_rows, gate_weight, preferred_element_type=jnp.float32)  17.2 us
    psum x1, blocking collectives, per_device(): lax.psum(jnp.sum(widened * widened, axis=-1, keepdims=True), 'head')  13.5 us
    dot_general x1, matrix products, per_device(): jnp.dot(attended, out_weight, preferred_element_type=jnp.float32)  9.62 us
  transfers between devices with their start and end apart: 4, of which 3 were waited for; matrix products, arithmetic and copies ran while one was open for 0% of the time, Pallas kernels for 0%

profile of v1, /device:TPU:1, one launch (start us, length us, event | category | flops | bytes accessed | tf_op | source)
XLA Modules:
  0.0 413.5 jit_solution(3300985366616468473)
XLA Ops:
  7.2 1.7 stack.2
  8.8 8.4 %all-to-all-start = ((bf16[16,128,128]{2,1,0:T(8,128)(2,1)}), bf16[16,128,128]{2,1,0:T(8,128)(2,1)S(1)}, u32[]{:S(2)}, u32[]{:S(2)}) async-start(bf16[16,128,128]{2,1,0:T(8,128)(2,1)} %stack.2), calls=%async_computation | async-start | bytes 1048576 | tf_op jit(solution)/shard_map/all_to_all | solution.py:74
  17.3 0.0 reduce-scatter.2.cloned.1.call-start
  17.3 0.6 slice.3
  18.5 26.8 %all_gather.9 = bf16[2048,128]{1,0:T(8,128)(2,1)S(1)} all-gather(bf16[128,128]{1,0:T(8,128)(2,1)} %param.11), channel_id=1, replica_groups=mesh['seq'=16,'head'=8] {'seq'}, dimensions={0}, use_global_device_ids=true | all-gather | bytes 557056 | tf_op jit(solution)/shard_map/all_gather | solution.py:72
  45.3 9.0 %conditional.1 = (f32[1,8,128]{2,1,0:T(8,128)S(1)}, f32[1,8,128,128]{2,3,1,0:T(8,128)S(1)}) conditional(s32[]{:T(128)} %bitcast.8, () %tuple.16, (s32[128]{0:T(128)S(1)}, s32[2048]{0:T(1024)S(1)}, bf16[128,1024]{1,0:T(8,128)(2,1)}, bf16[2048,128]{1,0:T(8,128)(2,1)S(1)}, bf16[16,128,128]{2,1,0:T(8,128)(2,1)S(1)}) %tuple.17), branch_computations={%region_0.0_spmd, %region_1.4_spmd} | conditional | flops 3779329024 | bytes 28082704 | solution.py:35
  45.3 0.3 broadcast_compare_fusion
  45.7 2.3 fusion.3
  48.0 4.6 %fusion.8 = f32[1,8,128,128]{2,3,1,0:T(8,128)S(1)} fusion(bf16[2048,128,1]{1,0,2:T(8,128)(2,1)S(1)} %bitcast.55, f32[2048,128,8]{1,0,2:T(8,128)S(1)} %get-tuple-element.30, f32[8,128]{1,0:T(8,128)S(1)} %broadcast_maximum_fusion, pred[128,2048]{0,1:T(8,128)(4,1)S(1)} %broadcast_compare_fusion), kind=kOutput, calls=%fused_computation.10 | convolution fusion | flops 3227516928 | bytes 9703424 | tf_op jit(solution)/shard_map/cond/branch_1_fun/kgrn,nkd->kgrd/dot_general | solution.py:20
  52.6 1.7 fusion.2
  54.3 0.1 divide_convert_fusion
  54.3 9.6 %convolution_convert_fusion = bf16[128,8192]{1,0:T(8,128)(2,1)} fusion(bf16[128,1024]{0,1:T(8,128)(2,1)S(1)} %bitcast.54, bf16[1024,8192]{1,0:T(8,128)(2,1)} %param.13), kind=kOutput, calls=%fused_computation.19 | convolution fusion | flops 2148532224 | bytes 19136512 | tf_op jit(solution)/shard_map/dot_general | solution.py:90
  64.0 0.0 reduce-scatter.2.cloned.1.call-update
  64.0 0.0 all-gather.3.cloned.1.call-start
  64.1 0.7 dynamic_slice.3
  64.7 49.8 %reduce-scatter.2.cloned.1.call-done = bf16[128,1024]{1,0:T(8,128)(2,1)} async-done(((bf16[128,8192]{1,0:T(8,128)(2,1)}), bf16[128,1024]{1,0:T(8,128)(2,1)}) %reduce-scatter.2.cloned.1.call-update) | async-done | bytes 262160 | tf_op jit(solution)/shard_map/reduce_scatter | solution.py:94
  114.5 1.1 fusion.18
  115.6 13.5 %psum.7 = f32[128,1]{0,1:T(1,128)S(1)} all-reduce(f32[128,1]{0,1:T(1,128)S(1)} %bitcast.58), channel_id=1, replica_groups=mesh['seq'=16,'head'=8] {'head'}, use_global_device_ids=true, to_apply=%region_6.7 | all-reduce | flops 128 | bytes 1024 | tf_op jit(solution)/shard_map/psum | solution.py:99
  129.2 0.8 fusion.20
  130.0 0.0 all-gather.5.cloned.1.call-start
  130.1 54.2 %all-gather.3.cloned.1.call-done = bf16[128,8192]{1,0:T(8,128)(2,1)} async-done(((bf16[128,1024]{1,0:T(8,128)(2,1)}), bf16[128,8192]{1,0:T(8,128)(2,1)}) %all-gather.3.cloned.1.call-update) | async-done | bytes 2097168 | tf_op jit(solution)/shard_map/all_gather | solution.py:104
  184.3 188.1 %all-gather.5.cloned.1.call-done = bf16[2048,8192]{1,0:T(8,128)(2,1)} async-done(((bf16[128,8192]{1,0:T(8,128)(2,1)}), bf16[2048,8192]{1,0:T(8,128)(2,1)}) %all-gather.5.cloned.1.call-update) | async-done | bytes 33554448 | tf_op jit(solution)/shard_map/all_gather | solution.py:105
  372.4 17.2 %fusion.21 = f32[2048,224]{0,1:T(8,128)S(1)} fusion(bf16[2048,8192]{1,0:T(8,128)(2,1)} %all-gather.5.cloned.1.call-done, bf16[8192,224]{0,1:T(8,128)(2,1)} %param.16), kind=kOutput, calls=%fused_computation.31 | convolution fusion | flops 7516192768 | bytes 39059456 | tf_op jit(solution)/shard_map/dot_general | solution.py:106
  389.7 17.3 %fusion.17 = bf16[2048,224]{0,1:T(8,128)(2,1)} fusion(bf16[2048,8192]{1,0:T(8,128)(2,1)} %all-gather.5.cloned.1.call-done, bf16[8192,224]{0,1:T(8,128)(2,1)S(1)} %copy-done.2, f32[2048,224]{0,1:T(8,128)S(1)} %fusion.21), kind=kOutput, calls=%fused_computation.21 | convolution fusion | flops 7518945280 | bytes 39976960 | tf_op jit(solution)/shard_map/dot_general | solution.py:107
  (13 shorter events, 0.1 us)
Async XLA Ops:
  8.8 36.5 %all-to-all-start = ((bf16[16,128,128]{2,1,0:T(8,128)(2,1)}), bf16[16,128,128]{2,1,0:T(8,128)(2,1)S(1)}, u32[]{:S(2)}, u32[]{:S(2)}) async-start(bf16[16,128,128]{2,1,0:T(8,128)(2,1)} %stack.2), calls=%async_computation | async-start | bytes 1048576 | tf_op jit(solution)/shard_map/all_to_all | solution.py:74
  17.3 97.3 %reduce-scatter.2.cloned.1.call-start = ((), (), s32[]{:S(2)}) async-start(), calls=%async_computation.2 | async-start | bytes 2359296 | tf_op jit(solution)/shard_map/reduce_scatter | solution.py:94
  54.3 60.2 %copy-start.1 = (bf16[128,1024]{1,0:T(8,128)(2,1)S(1)}, bf16[128,1024]{1,0:T(8,128)(2,1)}, u32[]{:S(2)}) copy-start(bf16[128,1024]{1,0:T(8,128)(2,1)} %param.14) | copy-start | bytes 786436
  64.0 120.3 %all-gather.3.cloned.1.call-start = ((), (), s32[]{:S(2)}) async-start(), calls=%async_computation.3 | async-start | bytes 2359296 | tf_op jit(solution)/shard_map/all_gather | solution.py:104
  115.6 274.0 %copy-start = (bf16[128,1024]{1,0:T(8,128)(2,1)}, bf16[128,1024]{1,0:T(8,128)(2,1)S(1)}, u32[]{:S(2)}) copy-start(bf16[128,1024]{1,0:T(8,128)(2,1)S(1)} %get-tuple-element.28) | copy-start | bytes 786436
  130.0 242.4 %all-gather.5.cloned.1.call-start = ((), (), s32[]{:S(2)}) async-start(), calls=%async_computation.4 | async-start | bytes 35651584 | tf_op jit(solution)/shard_map/all_gather | solution.py:105
  372.4 17.3 %copy-start.2 = (bf16[8192,224]{0,1:T(8,128)(2,1)S(1)}, bf16[8192,224]{0,1:T(8,128)(2,1)}, u32[]{:S(2)}) copy-start(bf16[8192,224]{0,1:T(8,128)(2,1)} %param.17) | copy-start | bytes 11010052
Sparse Core Ops, SparseCore 0:
  64.1 50.3 reduce-scatter.1
  130.2 54.0 all-gather.2
  186.8 185.5 all-gather.4
